TPU v7x, 256 devices: a whole 4x4x8 slice. The times are simulated.
256 devices in a mesh: batch: 4 (over x), blk: 4 (over z_hi, core), uly: 16 (over y, z_lo).
Axes of the slice: x: 4, y: 4, z: 8 (z_hi: 2, z_lo: 4; z = z_hi * 4 + z_lo), core: 2. Of those that a mesh axis runs over, the one named last changes fastest.
Arguments:
- queries: bfloat16 [32768, 4096], P(('batch', 'blk', 'uly')), parts along dimension 0, may hold values from -6 to 6
- keys: bfloat16 [32768, 512], P(('batch', 'blk', 'uly')), parts along dimension 0, may hold values from -6 to 6
- values: bfloat16 [32768, 512], P(('batch', 'blk', 'uly')), parts along dimension 0, may hold values from -6 to 6
- saved_out: bfloat16 [32768, 4096], P(('batch', 'blk', 'uly')), parts along dimension 0, may hold values from -6 to 6
- out_grad: bfloat16 [32768, 4096], P(('batch', 'blk', 'uly')), parts along dimension 0, may hold values from -6 to 6
- doc_lengths: int32 [32], P('batch'), parts along dimension 0, may hold values from 1 to 4096, 8192 in all
Outputs:
- gradient_of_queries: bfloat16 [32768, 4096], P(('batch', 'blk', 'uly')), parts along dimension 0
- gradient_of_keys: bfloat16 [32768, 512], P(('batch', 'blk', 'uly')), parts along dimension 0
- gradient_of_values: bfloat16 [32768, 512], P(('batch', 'blk', 'uly')), parts along dimension 0
There are 4 independent parts, one for each index of `batch`. A program takes and returns all parts, laid end to end along the dimension named above; each array names one. Nothing has to cross between parts.
Inputs may be any that keep to these rules, and one draw needn't show every extreme that they name: `doc_lengths`: the lengths sum to 8192 and the largest is exactly 4096.
All inputs are finite; a program needn't handle non-finite values.
Results may differ from a plain program's by a relative error of at most 0.0054.
Values may be sent and summed in bfloat16 or wider, within the bound.
No kernel may reach another device: no remote copies, remote signals or barrier semaphores. Data moves between devices by JAX's collectives and lax.ppermute only.
A program may use at most 64 MiB of HBM per device.

v0:
```python
import jax
import jax.numpy as jnp
import numpy as np
from jax import lax
from jax.sharding import PartitionSpec as P

HEAD_SIZE = 128
BLOCK = 512


def in_one_piece(arrays, axis, split_dim, concat_dim, along):
    ends, at = ([], 0)
    for a in arrays[:-1]:
        at += a.shape[along]
        ends.append(at)
    both = jnp.concatenate(arrays, axis=along)
    return tuple(
        jnp.split(
            lax.all_to_all(both, axis, split_axis=split_dim, concat_axis=concat_dim, tiled=True),
            ends,
            axis=along,
        )
    )


def passed_along(shard, axis, by):
    peers = lax.axis_size(axis)
    pairs = [(i, i + by) for i in range(peers) if 0 <= i + by < peers]
    return lax.ppermute(shard, axis, pairs)


def cut_along(shard, dim, peers):
    dims = shard.shape
    tiles = shard.reshape(*dims[:dim], peers, dims[dim] // peers, *dims[dim + 1 :])
    return jnp.moveaxis(tiles, dim, 0)


def piece_ends(length, count):
    unit = 8 if length >= 8 * count else 1
    return [length // unit * k // count * unit for k in range(1, count)]


def in_order(tiles, dim):
    tiles = jnp.moveaxis(tiles, 0, dim)
    dims = tiles.shape
    return tiles.reshape(*dims[:dim], dims[dim] * dims[dim + 1], *dims[dim + 2 :])


def several_exchanges(shard, axis, pieces, split_dim, concat_dim):
    tiles = cut_along(shard, split_dim, lax.axis_size(axis))
    split_at = max(range(1, max(2, tiles.ndim - 1)), key=lambda d: tiles.shape[d])
    gathered = []
    for section in jnp.split(tiles, piece_ends(tiles.shape[split_at], pieces), axis=split_at):
        if section.size:
            gathered.append(lax.all_to_all(section, axis, split_axis=0, concat_axis=0, tiled=True))
    return in_order(jnp.concatenate(gathered, axis=split_at), concat_dim)


def on_device(queries, keys, values, saved_out, out_grad, doc_lengths):
    width = lax.axis_size("uly")
    blk_index = lax.axis_index("blk")
    rows = queries.shape[0]
    head_dim = HEAD_SIZE
    q_heads = queries.shape[1] // head_dim
    kv_heads = keys.shape[1] // head_dim
    group_width = q_heads // kv_heads
    per_device = q_heads // width
    kv_local = max(1, per_device // group_width)
    group_local = min(group_width, per_device)
    slab = width * rows
    window = slab // 2
    tile = BLOCK
    tiles = slab // tile
    reach = tile + window
    softmax_scale = head_dim ** (-0.5)
    products = jnp.sum(
        out_grad.astype(jnp.float32).reshape(rows, q_heads, head_dim)
        * saved_out.astype(jnp.float32).reshape(rows, q_heads, head_dim),
        axis=2,
    )
    delta_rows = products.astype(jnp.bfloat16)
    moved = in_one_piece(
        (
            queries.reshape(rows, width, per_device * head_dim),
            out_grad.reshape(rows, width, per_device * head_dim),
            delta_rows.reshape(rows, width, per_device),
        ),
        "uly",
        1,
        0,
        2,
    )
    query_heads = moved[0].reshape(slab, kv_local, group_local, head_dim)
    grad_heads = moved[1].reshape(slab, kv_local, group_local, head_dim)
    delta_heads = moved[2].astype(jnp.float32).transpose(1, 2, 0)
    table = np.array(
        [
            unit * per_device // group_width + offset
            for unit in range(width)
            for offset in range(kv_local)
        ],
        dtype=np.int32,
    )
    key_copy = keys.reshape(rows, kv_heads, head_dim)[:, table, :].reshape(
        rows, width, kv_local * head_dim
    )
    value_copy = values.reshape(rows, kv_heads, head_dim)[:, table, :].reshape(
        rows, width, kv_local * head_dim
    )
    key_mine, value_mine = in_one_piece((key_copy, value_copy), "uly", 1, 0, 2)
    key_mine = key_mine.reshape(slab, kv_local * head_dim)
    value_mine = value_mine.reshape(slab, kv_local * head_dim)
    rim_keys, rim_values = passed_along(
        (key_mine[slab - window :], value_mine[slab - window :]), "blk", 1
    )
    key_ext = jnp.concatenate([rim_keys, key_mine], axis=0).reshape(
        window + slab, kv_local, head_dim
    )
    value_ext = jnp.concatenate([rim_values, value_mine], axis=0).reshape(
        window + slab, kv_local, head_dim
    )
    bounds = jnp.cumsum(doc_lengths)[:-1]

    def document(positions):
        return jnp.sum((positions[:, None] >= bounds[None, :]).astype(jnp.int32), axis=1)

    slab_start = blk_index * slab

    def step(turn, carry):
        query_total, key_total, value_total = carry
        first = (turn * tile).astype(jnp.int32)
        query_tile = lax.dynamic_slice_in_dim(query_heads, first, tile, 0)
        grad_tile = lax.dynamic_slice_in_dim(grad_heads, first, tile, 0)
        delta_tile = lax.dynamic_slice_in_dim(delta_heads, first, tile, 2)
        key_tile = lax.dynamic_slice_in_dim(key_ext, first, reach, 0)
        value_tile = lax.dynamic_slice_in_dim(value_ext, first, reach, 0)
        query_pos = slab_start + first + jnp.arange(tile, dtype=jnp.int32)
        key_pos = slab_start - window + first + jnp.arange(reach, dtype=jnp.int32)
        qp = query_pos[:, None]
        kp = key_pos[None, :]
        allowed = (
            (kp <= qp)
            & (kp > qp - window)
            & (kp >= 0)
            & (document(jnp.maximum(key_pos, 0))[None, :] == document(query_pos)[:, None])
        )
        attention_logits = (
            jnp.einsum("qagd,kad->agqk", query_tile, key_tile, preferred_element_type=jnp.float32)
            * softmax_scale
        )
        peak = jnp.max(jnp.where(allowed, attention_logits, -1e30), axis=-1, keepdims=True)
        total = jnp.sum(
            jnp.where(allowed, jnp.exp(attention_logits - peak), 0.0), axis=-1, keepdims=True
        )
        log_total = peak + jnp.log(total)
        probs = jnp.where(allowed, jnp.exp(attention_logits - log_total), 0.0)
        probability_lowered = probs.astype(jnp.bfloat16)
        value_part = jnp.einsum(
            "agqk,qagd->kad", probability_lowered, grad_tile, preferred_element_type=jnp.float32
        )
        probability_gradient = jnp.einsum(
            "qagd,kad->agqk", grad_tile, value_tile, preferred_element_type=jnp.float32
        )
        score_gradient = (probs * (probability_gradient - delta_tile[..., None])).astype(
            jnp.bfloat16
        )
        query_part = (
            jnp.einsum(
                "agqk,kad->qagd", score_gradient, key_tile, preferred_element_type=jnp.float32
            )
            * softmax_scale
        )
        key_part = (
            jnp.einsum(
                "agqk,qagd->kad", score_gradient, query_tile, preferred_element_type=jnp.float32
            )
            * softmax_scale
        )
        query_total = lax.dynamic_update_slice_in_dim(query_total, query_part, first, 0)
        key_total = lax.dynamic_update_slice_in_dim(
            key_total, lax.dynamic_slice_in_dim(key_total, first, reach, 0) + key_part, first, 0
        )
        value_total = lax.dynamic_update_slice_in_dim(
            value_total,
            lax.dynamic_slice_in_dim(value_total, first, reach, 0) + value_part,
            first,
            0,
        )
        return (query_total, key_total, value_total)

    start_state = (
        jnp.zeros((slab, kv_local, group_local, head_dim), jnp.float32),
        jnp.zeros((window + slab, kv_local, head_dim), jnp.float32),
        jnp.zeros((window + slab, kv_local, head_dim), jnp.float32),
    )
    query_total, key_ext_grad, value_ext_grad = lax.fori_loop(0, tiles, step, start_state)
    back_keys, back_values = passed_along(
        (key_ext_grad[:window], value_ext_grad[:window]), "blk", -1
    )
    lead = jnp.zeros((slab - window, kv_local, head_dim), jnp.float32)
    key_total = key_ext_grad[window:] + jnp.concatenate([lead, back_keys], axis=0)
    value_total = value_ext_grad[window:] + jnp.concatenate([lead, back_values], axis=0)
    query_low = query_total.astype(jnp.bfloat16).reshape(slab, 1, per_device * head_dim)
    query_back = several_exchanges(query_low, "uly", 2, 0, 1).reshape(rows, q_heads * head_dim)
    copies = width * kv_local // kv_heads
    key_back, value_back = in_one_piece((key_total, value_total), "uly", 0, 1, 2)
    key_result = (
        key_back.reshape(rows, kv_heads, copies, head_dim)
        .sum(axis=2)
        .reshape(rows, kv_heads * head_dim)
    )
    value_result = (
        value_back.reshape(rows, kv_heads, copies, head_dim)
        .sum(axis=2)
        .reshape(rows, kv_heads * head_dim)
    )
    return (query_back, key_result.astype(jnp.bfloat16), value_result.astype(jnp.bfloat16))


def solution(mesh):
    return jax.shard_map(
        on_device,
        mesh=mesh,
        in_specs=(
            P(("batch", "blk", "uly"), None),
            P(("batch", "blk", "uly"), None),
            P(("batch", "blk", "uly"), None),
            P(("batch", "blk", "uly"), None),
            P(("batch", "blk", "uly"), None),
            P("batch"),
        ),
        out_specs=(
            P(("batch", "blk", "uly"), None),
            P(("batch", "blk", "uly"), None),
            P(("batch", "blk", "uly"), None),
        ),
        check_vma=False,
    )
```

profile of v0, /device:TPU:1, one launch (start us, length us, event | category | flops | bytes accessed | tf_op | source)
XLA Modules:
  0.0 278.4 jit_solution(18202995333392024633)
XLA Ops:
  6.1 9.3 %all-to-all-start = ((bf16[128,16,256]{2,0,1:T(8,128)(2,1)}), bf16[128,16,256]{2,0,1:T(8,128)(2,1)S(1)}, u32[]{:S(2)}, u32[]{:S(2)}) async-start(bf16[128,16,256]{2,0,1:T(8,128)(2,1)} %pad_maximum_fusion.2), calls=%async_computation | async-start | bytes 2097152 | tf_op jit(solution)/shard_map/all_to_all | solution.py:19
  19.4 3.1 %pad_maximum_fusion = bf16[128,16,514]{0,2,1:T(8,128)(2,1)} fusion(bf16[128,16,2]{0,2,1:T(2,128)(2,1)S(1)} %bitcast.248, bf16[128,16,256]{0,2,1:T(8,128)(2,1)} %bitcast.240, bf16[128,16,256]{0,2,1:T(8,128)(2,1)} %bitcast.239), kind=kLoop, calls=%fused_computation.62 | loop fusion | flops 6316032 | bytes 4210688 | tf_op jit(solution)/shard_map/concatenate | solution.py:16
  22.4 20.0 %all-to-all-done = bf16[128,16,256]{2,0,1:T(8,128)(2,1)S(1)} async-done(((bf16[128,16,256]{2,0,1:T(8,128)(2,1)}), bf16[128,16,256]{2,0,1:T(8,128)(2,1)S(1)}, u32[]{:S(2)}, u32[]{:S(2)}) %all-to-all-start) | async-done | bytes 1048608 | tf_op jit(solution)/shard_map/all_to_all | solution.py:19
  42.4 4.4 %all-to-all-start.1 = ((bf16[128,16,514]{0,2,1:T(8,128)(2,1)}), bf16[128,16,514]{0,2,1:T(8,128)(2,1)}, u32[]{:S(2)}, u32[]{:S(2)}) async-start(bf16[128,16,514]{0,2,1:T(8,128)(2,1)} %pad_maximum_fusion), calls=%async_computation.1 | async-start | bytes 4259840 | tf_op jit(solution)/shard_map/all_to_all | solution.py:19
  47.1 7.7 %collective-permute-start.1 = (bf16[1024,128]{1,0:T(8,128)(2,1)S(1)}, bf16[1024,128]{1,0:T(8,128)(2,1)S(1)}, u32[]{:S(2)}, u32[]{:S(2)}) collective-permute-start(bf16[1024,128]{1,0:T(8,128)(2,1)S(1)} %get-tuple-element.425), channel_id=1, source_target_pairs={{0,16},{16,32},{32,48},{1,17},{17,33},{33,49},{2,18},{18,34},{34,5... | collective-permute-start | bytes 786440 | tf_op jit(solution)/shard_map/ppermute | solution.py:29
  54.8 2.1 collective-permute-start
  57.0 27.5 %collective-permute-done.1 = bf16[1024,128]{1,0:T(8,128)(2,1)S(1)} collective-permute-done((bf16[1024,128]{1,0:T(8,128)(2,1)S(1)}, bf16[1024,128]{1,0:T(8,128)(2,1)S(1)}, u32[]{:S(2)}, u32[]{:S(2)}) %collective-permute-start.1) | collective-permute-done | bytes 262176 | tf_op jit(solution)/shard_map/ppermute | solution.py:29
  85.5 1.9 collective-permute-done
  87.4 15.7 %all-to-all-done.1 = bf16[128,16,514]{0,2,1:T(8,128)(2,1)} async-done(((bf16[128,16,514]{0,2,1:T(8,128)(2,1)}), bf16[128,16,514]{0,2,1:T(8,128)(2,1)}, u32[]{:S(2)}, u32[]{:S(2)}) %all-to-all-start.1) | async-done | bytes 2105376 | tf_op jit(solution)/shard_map/all_to_all | solution.py:19
  103.0 3.2 %copy.148 = bf16[16,128,1,514]{1,0,3,2:T(8,128)(2,1)} copy(bf16[16,128,1,514]{1,3,0,2:T(8,128)(2,1)} %bitcast.41) | data formatting | bytes 4210688 | tf_op jit(solution)/shard_map/all_to_all | solution.py:19
  106.3 4.4 %all_to_all.52 = bf16[2048,1,514]{0,2,1:T(8,128)(2,1)} reshape(bf16[16,128,1,514]{1,0,3,2:T(8,128)(2,1)} %copy.148) | data formatting | bytes 4210688 | tf_op jit(solution)/shard_map/all_to_all | solution.py:19
  111.4 2.7 fusion.53
  116.6 44.4 %while.20 = (s32[]{:T(128)}, bf16[2048,1,2,128]{0,3,2,1:T(8,128)(2,1)}, f32[3072,1,128]{0,2,1:T(8,128)S(1)}, f32[3072,1,128]{0,2,1:T(8,128)}, bf16[3072,1,128]{2...) while((s32[]{:T(128)}, ...), condition=%wide.region_7.8_spmd, body=%wide.region_2.7_spmd.sunk | while | flops 2045491200 | bytes 72844824 | solution.py:196
  116.9 1.5 compare_and_fusion.2
  121.5 1.9 fusion.86
  123.5 2.4 fusion.83
  128.0 1.5 compare_and_fusion.2
  132.6 1.9 fusion.86
  134.6 2.4 fusion.83
  139.1 1.5 compare_and_fusion.2
  143.7 1.9 fusion.86
  145.7 2.4 fusion.83
  150.2 1.5 compare_and_fusion.2
  153.1 1.4 fusion.82
  154.8 1.9 fusion.86
  156.8 2.4 fusion.83
  161.0 1.5 copy.181
  162.5 1.8 fusion.54
  164.3 2.9 %copy.178 = bf16[16,64,1,256]{3,1,2,0:T(8,128)(2,1)} copy(bf16[16,64,1,256]{1,0,3,2:T(8,128)(2,1)} %get-tuple-element.423) | data formatting | bytes 1048576
  167.2 4.4 %all-to-all-start.2 = ((bf16[16,64,1,256]{3,1,2,0:T(8,128)(2,1)}), bf16[16,64,1,256]{3,1,2,0:T(8,128)(2,1)}, u32[]{:S(2)}, u32[]{:S(2)}) async-start(bf16[16,64,1,256]{3,1,2,0:T(8,128)(2,1)} %copy.178), calls=%async_computation.2 | async-start | bytes 1048576 | tf_op jit(solution)/shard_map/all_to_all | solution.py:55
  172.4 1.9 copy.155
  174.4 3.2 %collective-permute-start.2 = (f32[1024,1,128]{2,1,0:T(1,128)}, f32[1024,1,128]{2,1,0:T(1,128)}, u32[]{:S(2)}, u32[]{:S(2)}) collective-permute-start(f32[1024,1,128]{2,1,0:T(1,128)} %copy.155), channel_id=1, source_target_pairs={{16,0},{32,16},{48,32},{17,1},{33,17},{49,33},{18,2},{34,18},{50,3... | collective-permute-start | bytes 1572872 | tf_op jit(solution)/shard_map/ppermute | solution.py:29
  178.4 1.9 copy.157
  180.3 1.9 collective-permute-start.3
  182.2 2.8 %copy.156 = f32[3072,1,128]{2,1,0:T(1,128)} copy(f32[3072,1,128]{0,2,1:T(8,128)S(1)} %copy-done.2) | data formatting | bytes 3145728 | tf_op jit(solution)/shard_map/while | solution.py:196
  185.0 1.6 copy.154
  186.7 2.8 copy.179
  189.5 7.5 %all-to-all-start.3 = ((bf16[16,64,1,256]{3,1,2,0:T(8,128)(2,1)}), bf16[16,64,1,256]{3,1,2,0:T(8,128)(2,1)}, u32[]{:S(2)}, u32[]{:S(2)}) async-start(bf16[16,64,1,256]{3,1,2,0:T(8,128)(2,1)} %copy.179), calls=%async_computation.3 | async-start | bytes 1048576 | tf_op jit(solution)/shard_map/all_to_all | solution.py:55
  197.0 2.1 slice_add_fusion.1
  199.1 2.1 slice_add_fusion
  201.2 3.0 %pad_maximum_fusion.1 = f32[2048,1,256]{2,1,0:T(1,128)} fusion(f32[2048,1,128]{2,1,0:T(1,128)S(1)} %slice_add_fusion, f32[2048,1,128]{2,1,0:T(1,128)S(1)} %slice_add_fusion.1), kind=kLoop, calls=%fused_computation.63 | loop fusion | flops 524288 | bytes 4194304 | tf_op jit(solution)/shard_map/concatenate | solution.py:16
  204.2 18.2 %all-to-all-done.3 = bf16[16,64,1,256]{3,1,2,0:T(8,128)(2,1)} async-done(((bf16[16,64,1,256]{3,1,2,0:T(8,128)(2,1)}), bf16[16,64,1,256]{3,1,2,0:T(8,128)(2,1)}, u32[]{:S(2)}, u32[]{:S(2)}) %all-to-all-start.3) | async-done | bytes 524320 | tf_op jit(solution)/shard_map/all_to_all | solution.py:55
  222.4 3.7 %all-to-all-start.4 = ((f32[2048,1,256]{2,1,0:T(1,128)}), f32[2048,1,256]{2,1,0:T(1,128)S(1)}, u32[]{:S(2)}, u32[]{:S(2)}) async-start(f32[2048,1,256]{2,1,0:T(1,128)} %pad_maximum_fusion.1), calls=%async_computation.4 | async-start | bytes 4194304 | tf_op jit(solution)/shard_map/all_to_all | solution.py:19
  226.1 1.5 copy.152
  227.7 2.4 copy.153
  230.0 2.8 %pad_maximum_fusion.3 = bf16[16,128,1,256]{1,3,0,2:T(8,128)(2,1)} fusion(bf16[16,64,1,256]{1,3,0,2:T(8,128)(2,1)} %copy.153, bf16[16,64,1,256]{1,3,0,2:T(8,128)(2,1)S(1)} %copy.152), kind=kLoop, calls=%fused_computation.69 | loop fusion | flops 2097152 | bytes 2097152 | tf_op jit(solution)/shard_map/concatenate | solution.py:56
  232.8 2.3 copy.162
  235.1 41.1 %all-to-all-done.4 = f32[2048,1,256]{2,1,0:T(1,128)S(1)} async-done(((f32[2048,1,256]{2,1,0:T(1,128)}), f32[2048,1,256]{2,1,0:T(1,128)S(1)}, u32[]{:S(2)}, u32[]{:S(2)}) %all-to-all-start.4) | async-done | bytes 2097184 | tf_op jit(solution)/shard_map/all_to_all | solution.py:19
  (138 shorter events, 36.6 us)
Async XLA Ops:
  4.9 10.4 %copy-start.7 = (bf16[128,4096]{1,0:T(8,128)(2,1)S(1)}, bf16[128,4096]{1,0:T(8,128)(2,1)}, u32[]{:S(2)}) copy-start(bf16[128,4096]{1,0:T(8,128)(2,1)} %param.11) | copy-start | bytes 3145732
  6.1 10.6 %copy-start.6 = (bf16[128,4096]{1,0:T(8,128)(2,1)S(1)}, bf16[128,4096]{1,0:T(8,128)(2,1)}, u32[]{:S(2)}) copy-start(bf16[128,4096]{1,0:T(8,128)(2,1)} %param.15) | copy-start | bytes 3145732
  6.1 36.4 %all-to-all-start = ((bf16[128,16,256]{2,0,1:T(8,128)(2,1)}), bf16[128,16,256]{2,0,1:T(8,128)(2,1)S(1)}, u32[]{:S(2)}, u32[]{:S(2)}) async-start(bf16[128,16,256]{2,0,1:T(8,128)(2,1)} %pad_maximum_fusion.2), calls=%async_computation | async-start | bytes 2097152 | tf_op jit(solution)/shard_map/all_to_all | solution.py:19
  16.7 1.3 copy-start.8
  22.4 24.5 %copy-start.11 = (s32[8]{0:T(128)S(1)}, s32[8]{0:T(128)}, u32[]{:S(2)}) copy-start(s32[8]{0:T(128)} %param.16) | copy-start | bytes 100
  42.4 60.6 %all-to-all-start.1 = ((bf16[128,16,514]{0,2,1:T(8,128)(2,1)}), bf16[128,16,514]{0,2,1:T(8,128)(2,1)}, u32[]{:S(2)}, u32[]{:S(2)}) async-start(bf16[128,16,514]{0,2,1:T(8,128)(2,1)} %pad_maximum_fusion), calls=%async_computation.1 | async-start | bytes 4259840 | tf_op jit(solution)/shard_map/all_to_all | solution.py:19
  47.1 37.4 %collective-permute-start.1 = (bf16[1024,128]{1,0:T(8,128)(2,1)S(1)}, bf16[1024,128]{1,0:T(8,128)(2,1)S(1)}, u32[]{:S(2)}, u32[]{:S(2)}) collective-permute-start(bf16[1024,128]{1,0:T(8,128)(2,1)S(1)} %get-tuple-element.425), channel_id=1, source_target_pairs={{0,16},{16,32},{32,48},{1,17},{17,33},{33,49},{2,18},{18,34},{34,5... | collective-permute-start | bytes 786440 | tf_op jit(solution)/shard_map/ppermute | solution.py:29
  54.8 32.5 %collective-permute-start = (bf16[1024,128]{1,0:T(8,128)(2,1)S(1)}, bf16[1024,128]{1,0:T(8,128)(2,1)S(1)}, u32[]{:S(2)}, u32[]{:S(2)}) collective-permute-start(bf16[1024,128]{1,0:T(8,128)(2,1)S(1)} %get-tuple-element.426), channel_id=1, source_target_pairs={{0,16},{16,32},{32,48},{1,17},{17,33},{33,49},{2,18},{18,34},{34,5... | collective-permute-start | bytes 786440 | tf_op jit(solution)/shard_map/ppermute | solution.py:29
  119.8 1.5 copy-start
  119.8 1.7 copy-start.9
  121.5 1.9 copy-start.10
  123.5 2.4 copy-start.1
  123.5 2.4 copy-start.4
  126.5 1.2 copy-start.5
  130.9 1.5 copy-start
  130.9 1.7 copy-start.9
  132.6 1.9 copy-start.10
  134.6 2.4 copy-start.1
  134.6 2.4 copy-start.4
  137.6 1.2 copy-start.5
  142.0 1.5 copy-start
  142.0 1.7 copy-start.9
  143.7 1.9 copy-start.10
  145.7 2.4 copy-start.1
  145.7 2.4 copy-start.4
  148.7 1.2 copy-start.5
  153.1 1.5 copy-start
  153.1 1.7 copy-start.9
  154.8 1.9 copy-start.10
  156.7 2.4 copy-start.1
  156.8 2.4 copy-start.4
  159.8 1.2 copy-start.5
  164.3 13.2 %copy-start.2 = (f32[3072,1,128]{0,2,1:T(8,128)S(1)}, f32[3072,1,128]{0,2,1:T(8,128)}, u32[]{:S(2)}) copy-start(f32[3072,1,128]{0,2,1:T(8,128)} %get-tuple-element.307) | copy-start | bytes 4718596
  167.2 22.2 %all-to-all-start.2 = ((bf16[16,64,1,256]{3,1,2,0:T(8,128)(2,1)}), bf16[16,64,1,256]{3,1,2,0:T(8,128)(2,1)}, u32[]{:S(2)}, u32[]{:S(2)}) async-start(bf16[16,64,1,256]{3,1,2,0:T(8,128)(2,1)} %copy.178), calls=%async_computation.2 | async-start | bytes 1048576 | tf_op jit(solution)/shard_map/all_to_all | solution.py:55
  174.4 22.6 %collective-permute-start.2 = (f32[1024,1,128]{2,1,0:T(1,128)}, f32[1024,1,128]{2,1,0:T(1,128)}, u32[]{:S(2)}, u32[]{:S(2)}) collective-permute-start(f32[1024,1,128]{2,1,0:T(1,128)} %copy.155), channel_id=1, source_target_pairs={{16,0},{32,16},{48,32},{17,1},{33,17},{49,33},{18,2},{34,18},{50,3... | collective-permute-start | bytes 1572872 | tf_op jit(solution)/shard_map/ppermute | solution.py:29
  180.3 18.8 %collective-permute-start.3 = (f32[1024,1,128]{2,1,0:T(1,128)}, f32[1024,1,128]{2,1,0:T(1,128)}, u32[]{:S(2)}, u32[]{:S(2)}) collective-permute-start(f32[1024,1,128]{2,1,0:T(1,128)} %copy.157), channel_id=1, source_target_pairs={{16,0},{32,16},{48,32},{17,1},{33,17},{49,33},{18,2},{34,18},{50,3... | collective-permute-start | bytes 1572872 | tf_op jit(solution)/shard_map/ppermute | solution.py:29
  189.4 9.7 %copy-start.3 = (f32[3072,1,128]{2,1,0:T(1,128)S(1)}, f32[3072,1,128]{2,1,0:T(1,128)}, u32[]{:S(2)}) copy-start(f32[3072,1,128]{2,1,0:T(1,128)} %copy.156) | copy-start | bytes 4718596
  189.5 33.0 %all-to-all-start.3 = ((bf16[16,64,1,256]{3,1,2,0:T(8,128)(2,1)}), bf16[16,64,1,256]{3,1,2,0:T(8,128)(2,1)}, u32[]{:S(2)}, u32[]{:S(2)}) async-start(bf16[16,64,1,256]{3,1,2,0:T(8,128)(2,1)} %copy.179), calls=%async_computation.3 | async-start | bytes 1048576 | tf_op jit(solution)/shard_map/all_to_all | solution.py:55
  222.4 53.8 %all-to-all-start.4 = ((f32[2048,1,256]{2,1,0:T(1,128)}), f32[2048,1,256]{2,1,0:T(1,128)S(1)}, u32[]{:S(2)}, u32[]{:S(2)}) async-start(f32[2048,1,256]{2,1,0:T(1,128)} %pad_maximum_fusion.1), calls=%async_computation.4 | async-start | bytes 4194304 | tf_op jit(solution)/shard_map/all_to_all | solution.py:19
where the time goes:
time: 280 us; the launch traced here: 278 us
  waiting for transfers between devices  124 us (44%)
  local copies, waits for them, and re-layouts  47.6 us (17%)
  starting transfers between devices  44.2 us (16%)
  other arithmetic  30.5 us (11%)
  matrix products  29.9 us (11%)
    all_to_all x3, waiting for transfers between devices, in_one_piece(): lax.all_to_all(both, axis, split_axis=split_dim, concat_axis=concat_dim,...  76.8 us
    ppermute x4, waiting for transfers between devices, passed_along(): return lax.ppermute(shard, axis, pairs)  29.4 us
    all_to_all x2, waiting for transfers between devices, several_exchanges(): lax.all_to_all(section, axis, split_axis=0, concat_axis=0, tiled=True)  18.2 us
    all_to_all x3, starting transfers between devices, in_one_piece(): lax.all_to_all(both, axis, split_axis=split_dim, concat_axis=concat_dim,...  17.5 us
    unnamed x24, local copies, waits for them, and re-layouts  16.2 us
    ppermute x4, starting transfers between devices, passed_along(): return lax.ppermute(shard, axis, pairs)  14.9 us
    all_to_all x2, starting transfers between devices, several_exchanges(): lax.all_to_all(section, axis, split_axis=0, concat_axis=0, tiled=True)  11.9 us
    dot_general x4, matrix products, step(): jnp.einsum('qagd,kad->agqk', grad_tile, value_tile, preferred_element_typ...  9.51 us
  transfers between devices with their start and end apart: 9, of which 6 were waited for; matrix products, arithmetic and copies ran while one was open for 13% of the time, Pallas kernels for 0%

commit v1 on v0

v1 whole, which is shorter than its diff:
```python
import functools

import jax
import jax.numpy as jnp
import numpy as np
from jax import lax
from jax.experimental import pallas as pl
from jax.experimental.pallas import tpu as pltpu
from jax.sharding import Mesh
from jax.sharding import PartitionSpec as P

D = 128
T = 128
WINDOW = 1024
Y = 4
Z = 4
BACK = WINDOW // T
POS = BACK + Z * (Y - 1) + 1
ROWS = BACK // Z + Y
SPAN = (BACK + 1) * T
SCALE = D**-0.5
LOG2E = 1.4426950408889634
AXES = ("batch", "blk", "y", "z")


def pack_kv(k_ref, v_ref, o_ref):
    for h in range(Y):
        o_ref[h, :T] = k_ref[:, h * D : (h + 1) * D]
        o_ref[h, T:] = v_ref[:, h * D : (h + 1) * D]


def pack_rows(group, q_ref, s_ref, g_ref, qo_ref, go_ref):
    deltas = []
    for h in range(group):
        cols = slice(h * D, (h + 1) * D)
        qo_ref[0, h * T : (h + 1) * T] = q_ref[:, cols]
        grad = g_ref[:, cols]
        go_ref[0, h * T : (h + 1) * T] = grad
        product = grad.astype(jnp.float32) * s_ref[:, cols].astype(jnp.float32)
        deltas.append(jnp.sum(product.T, axis=0, keepdims=True))
    go_ref[0, group * T :] = jnp.concatenate(deltas, axis=0).astype(jnp.bfloat16)


def backward(
    group,
    doc_ref,
    q_ref,
    g_ref,
    x_ref,
    y1_ref,
    y2_ref,
    y3_ref,
    dq_ref,
    dx_ref,
    dy1_ref,
    dy2_ref,
    dy3_ref,
    k_scr,
    kt_scr,
    v_scr,
    dk_scr,
    dv_scr,
    s_scr,
    p_scr,
    ds_scr,
    delta_scr,
):
    k = pl.program_id(0)
    sources = (x_ref, y1_ref, y2_ref, y3_ref)

    @pl.when(k == 0)
    def _():
        for p in range(POS):
            m, d = divmod(p, Z)
            at = slice(p * T, (p + 1) * T)
            key = sources[d][m, :T]
            k_scr[at] = key
            kt_scr[:, at] = key.astype(jnp.float32).T.astype(jnp.bfloat16)
            v_scr[at] = sources[d][m, T:]
        dk_scr[...] = jnp.zeros_like(dk_scr)
        dv_scr[...] = jnp.zeros_like(dv_scr)

    delta_scr[...] = g_ref[0, group * T :, :].astype(jnp.float32)
    slab = Y * Z * T
    base = lax.axis_index("blk") * slab + (lax.axis_index("z") - BACK) * T
    first = pl.multiple_of(k * (Z * T), Z * T)
    query = first + WINDOW + lax.broadcasted_iota(jnp.int32, (1, T), 1)
    start = jnp.zeros((1, T), jnp.int32)
    bound = 0
    for c in range(7):
        bound = bound + doc_ref[c]
        start = jnp.where(query + base >= bound, bound, start)
    lowest = jnp.maximum(start - base, query - (WINDOW - 1)) - first
    lowest = jnp.concatenate([lowest, lowest], axis=1)
    key_at = lax.broadcasted_iota(jnp.int32, (T, 2 * T), 0)
    query_at = lax.broadcasted_iota(jnp.int32, (T, 2 * T), 1) & (T - 1)

    def pair(j, carry):
        at = pl.ds(pl.multiple_of(j * (2 * T), 2 * T), 2 * T)
        q2 = q_ref[0, at, :]
        g2 = g_ref[0, at, :]
        delta = jnp.concatenate(
            [
                delta_scr[pl.ds(2 * j, 1), :],
                delta_scr[pl.ds(2 * j + 1, 1), :],
            ],
            axis=1,
        )
        top = jnp.full((8, 2 * T), -1e30, jnp.float32)
        for c in range(BACK + 1):
            rows = slice(c * T, (c + 1) * T)
            keys = k_scr[pl.ds(pl.multiple_of(first + c * T, T), T), :]
            s = lax.dot_general(
                keys, q2, (((1,), (1,)), ((), ())), preferred_element_type=jnp.float32
            )
            allowed = key_at + c * T >= lowest
            if c == BACK:
                allowed = allowed & (key_at <= query_at)
            s = jnp.where(allowed, s, -1e30)
            s_scr[rows] = s
            for r in range(T // 8):
                top = jnp.maximum(top, s[r * 8 : (r + 1) * 8])
        peak = jnp.max(top, axis=0, keepdims=True) * (SCALE * LOG2E)
        total = jnp.zeros((8, 2 * T), jnp.float32)
        for c in range(BACK + 1):
            rows = slice(c * T, (c + 1) * T)
            e = jnp.exp2(s_scr[rows] * (SCALE * LOG2E) - peak)
            s_scr[rows] = e
            for r in range(T // 8):
                total = total + e[r * 8 : (r + 1) * 8]
        inverse = 1.0 / jnp.sum(total, axis=0, keepdims=True)
        for c in range(BACK + 1):
            rows = slice(c * T, (c + 1) * T)
            vals = v_scr[pl.ds(pl.multiple_of(first + c * T, T), T), :]
            dp = lax.dot_general(
                vals, g2, (((1,), (1,)), ((), ())), preferred_element_type=jnp.float32
            )
            p = s_scr[rows] * inverse
            p_scr[rows, at] = p.astype(jnp.bfloat16)
            ds_scr[rows, at] = (p * (dp - delta)).astype(jnp.bfloat16)
        return carry

    lax.fori_loop(0, group // 2, pair, 0)
    span = pl.ds(first, SPAN)
    dv_scr[span, :] += jnp.dot(
        p_scr[...], g_ref[0, : group * T, :], preferred_element_type=jnp.float32
    )
    dk_scr[span, :] += jnp.dot(
        ds_scr[...], q_ref[0], preferred_element_type=jnp.float32
    )
    dqt = jnp.dot(kt_scr[:, span], ds_scr[...], preferred_element_type=jnp.float32)
    for h in range(group):
        dq_ref[0, h * T : (h + 1) * T] = (
            (dqt[:, h * T : (h + 1) * T] * SCALE).T.astype(jnp.bfloat16)
        )

    @pl.when(k == Y - 1)
    def _():
        targets = (dx_ref, dy1_ref, dy2_ref, dy3_ref)
        for p in range(POS):
            m, d = divmod(p, Z)
            at = slice(p * T, (p + 1) * T)
            targets[d][m, :T] = (dk_scr[at] * SCALE).astype(targets[d].dtype)
            targets[d][m, T:] = dv_scr[at].astype(targets[d].dtype)


def combine(dx_ref, a_ref, b_ref, c_ref, own_ref, halo_ref, acc):
    z = lax.axis_index("z")
    acc[...] = dx_ref[...]
    for d, ref in ((1, a_ref), (2, b_ref), (3, c_ref)):
        off = (z < d).astype(jnp.int32)
        for m in range(ROWS - 1):
            acc[off + m] += ref[m].astype(jnp.float32)
    halo_ref[...] = acc[: BACK // Z].astype(jnp.bfloat16)
    own_ref[...] = acc[BACK // Z :]


def finish(own_ref, halo_ref, o_ref):
    for r in range(Y):
        total = own_ref[r]
        if r >= Y - BACK // Z:
            total = total + halo_ref[r - (Y - BACK // Z)].astype(jnp.float32)
        o_ref[r] = total.astype(jnp.bfloat16)


def vmem():
    return pl.BlockSpec(memory_space=pltpu.VMEM)


def on_device(queries, keys, values, saved_out, out_grad, doc_lengths):
    rows = queries.shape[0]
    group = queries.shape[1] // keys.shape[1]
    bf16, f32 = jnp.bfloat16, jnp.float32
    z = lax.axis_index("z")

    kv = pl.pallas_call(
        pack_kv,
        out_shape=jax.ShapeDtypeStruct((Y, 2 * T, D), bf16),
        in_specs=[vmem()] * 2,
        out_specs=vmem(),
    )(keys, values)
    own = lax.all_to_all(kv, "y", 0, 0, tiled=True)
    blks = lax.axis_size("blk")
    halo = lax.ppermute(
        own[Y - BACK // Z :], "blk", [(b, b + 1) for b in range(blks - 1)]
    )
    x = jnp.concatenate([halo, own], axis=0)

    wide = group * D
    q_out, g_out = pl.pallas_call(
        functools.partial(pack_rows, group),
        grid=(Y,),
        out_shape=(
            jax.ShapeDtypeStruct((Y, group * T, D), bf16),
            jax.ShapeDtypeStruct((Y, group * T + group, D), bf16),
        ),
        in_specs=[pl.BlockSpec((T, wide), lambda h: (0, h))] * 3,
        out_specs=(
            pl.BlockSpec((1, group * T, D), lambda h: (h, 0, 0)),
            pl.BlockSpec((1, group * T + group, D), lambda h: (h, 0, 0)),
        ),
    )(queries, saved_out, out_grad)
    q_all = lax.all_to_all(q_out, "y", 0, 0, tiled=True)
    g_all = lax.all_to_all(g_out, "y", 0, 0, tiled=True)

    def along(d):
        return [(i, (i - d) % Z) for i in range(Z)]

    def against(d):
        return [((i - d) % Z, i) for i in range(Z)]

    others = []
    for d in range(1, Z):
        part = lax.dynamic_slice_in_dim(x, (z < d).astype(jnp.int32), ROWS - 1, 0)
        others.append(lax.ppermute(part, "z", along(d)))

    def whole(shape):
        return pl.BlockSpec(shape, lambda k: (0,) * len(shape))

    part_shape = (ROWS - 1, 2 * T, D)
    x_shape = (ROWS, 2 * T, D)
    dq, dx, *dys = pl.pallas_call(
        functools.partial(backward, group),
        grid=(Y,),
        out_shape=(
            jax.ShapeDtypeStruct((Y, group * T, D), bf16),
            jax.ShapeDtypeStruct(x_shape, f32),
        )
        + (jax.ShapeDtypeStruct(part_shape, bf16),) * 3,
        in_specs=[
            pl.BlockSpec(memory_space=pltpu.SMEM),
            pl.BlockSpec((1, group * T, D), lambda k: (k, 0, 0)),
            pl.BlockSpec((1, group * T + group, D), lambda k: (k, 0, 0)),
            whole(x_shape),
        ]
        + [whole(part_shape)] * 3,
        out_specs=(pl.BlockSpec((1, group * T, D), lambda k: (k, 0, 0)), whole(x_shape))
        + (whole(part_shape),) * 3,
        scratch_shapes=[
            pltpu.VMEM((POS * T, D), bf16),
            pltpu.VMEM((D, POS * T), bf16),
            pltpu.VMEM((POS * T, D), bf16),
            pltpu.VMEM((POS * T, D), f32),
            pltpu.VMEM((POS * T, D), f32),
            pltpu.VMEM((SPAN, 2 * T), f32),
            pltpu.VMEM((SPAN, group * T), bf16),
            pltpu.VMEM((SPAN, group * T), bf16),
            pltpu.VMEM((group, T), f32),
        ],
        cost_estimate=pl.CostEstimate(
            flops=10 * Y * group * T * SPAN * D,
            transcendentals=Y * group * T * SPAN,
            bytes_accessed=8 << 20,
        ),
    )(doc_lengths, q_all, g_all, x, *others)

    dq_back = lax.all_to_all(dq, "y", 0, 0, tiled=True)
    dq_out = (
        dq_back.reshape(Y, group, T, D).transpose(2, 0, 1, 3).reshape(rows, Y * group * D)
    )

    backs = [lax.ppermute(dy, "z", against(d)) for d, dy in zip(range(1, Z), dys)]
    own_sum, halo_sum = pl.pallas_call(
        combine,
        out_shape=(
            jax.ShapeDtypeStruct((Y, 2 * T, D), f32),
            jax.ShapeDtypeStruct((BACK // Z, 2 * T, D), bf16),
        ),
        in_specs=[vmem()] * 4,
        out_specs=(vmem(), vmem()),
        scratch_shapes=[pltpu.VMEM(x_shape, f32)],
    )(dx, *backs)
    halo_back = lax.ppermute(halo_sum, "blk", [(b + 1, b) for b in range(blks - 1)])
    dkv = pl.pallas_call(
        finish,
        out_shape=jax.ShapeDtypeStruct((Y, 2 * T, D), bf16),
        in_specs=[vmem()] * 2,
        out_specs=vmem(),
    )(own_sum, halo_back)
    dkv = lax.all_to_all(dkv, "y", 0, 0, tiled=True)
    dkv = dkv.reshape(Y, 2, T, D).transpose(1, 2, 0, 3).reshape(2, rows, Y * D)
    return dq_out, dkv[0], dkv[1]


def solution(mesh):
    fine = Mesh(mesh.devices.reshape(4, 4, Y, Z), AXES)
    split = P(AXES, None)
    return jax.shard_map(
        on_device,
        mesh=fine,
        in_specs=(split,) * 5 + (P("batch"),),
        out_specs=(split,) * 3,
        check_vma=False,
    )
```

time: 280 us -> 165 us (0.59)
  the two profiles are of different devices: /device:TPU:1 before, /device:TPU:101 now
where the time goes in v1:
time: 165 us; the launch traced here: 164 us
  waiting for transfers between devices  77.1 us (47%)
  Pallas kernels  35.5 us (22%)
  starting transfers between devices  33.3 us (20%)
  blocking collectives  9.71 us (6%)
  local copies, waits for them, and re-layouts  7.45 us (5%)
    ppermute x3, waiting for transfers between devices, on_device(): lax.ppermute(dy, 'z', against(d))  27.4 us
    ppermute x3, waiting for transfers between devices, on_device(): others.append(lax.ppermute(part, 'z', along(d)))  25.6 us
    pallas_call x1, Pallas kernels, on_device(): pl.pallas_call(functools.partial(backward, group), grid=(Y,), out_shape=(...  25.3 us
    all_to_all x1, blocking collectives, on_device(): dkv = lax.all_to_all(dkv, 'y', 0, 0, tiled=True)  9.71 us
    all_to_all x1, waiting for transfers between devices, on_device(): dq_back = lax.all_to_all(dq, 'y', 0, 0, tiled=True)  9.55 us
    ppermute x1, waiting for transfers between devices, on_device(): lax.ppermute(halo_sum, 'blk', [(b + 1, b) for b in range(blks - 1)])  8.23 us
    ppermute x1, starting transfers between devices, on_device(): lax.ppermute(own[Y - BACK // Z:], 'blk', [(b, b + 1) for b in range(blks...  8.08 us
    ppermute x3, starting transfers between devices, on_device(): lax.ppermute(dy, 'z', against(d))  5.98 us
  transfers between devices with their start and end apart: 12, of which 8 were waited for; matrix products, arithmetic and copies ran while one was open for 1% of the time, Pallas kernels for 3%

profile of v1, /device:TPU:101, one launch (start us, length us, event | category | flops | bytes accessed | tf_op | source)
XLA Modules:
  0.0 163.8 jit_solution(13480552981089687364)
XLA Ops:
  0.6 1.7 %shard_map.86 = bf16[4,256,128]{2,1,0:T(8,128)(2,1)} custom-call(bf16[128,512]{1,0:T(8,128)(2,1)} %k_ref.1, bf16[128,512]{1,0:T(8,128)(2,1)} %v_ref.1), custom_call_target="tpu_custom_call" | custom-call | tf_op jit(solution)/shard_map/pallas_call | solution.py:196
  2.3 4.2 %all-to-all-start.2 = ((bf16[4,256,128]{2,1,0:T(8,128)(2,1)}), bf16[4,256,128]{2,1,0:T(8,128)(2,1)S(1)}, u32[]{:S(2)}, u32[]{:S(2)}) async-start(bf16[4,256,128]{2,1,0:T(8,128)(2,1)} %shard_map.86), calls=%async_computation.2 | async-start | bytes 524288 | tf_op jit(solution)/shard_map/all_to_all | solution.py:202
  6.5 4.2 %shard_map.85 = (bf16[4,1024,128]{2,1,0:T(8,128)(2,1)}, bf16[4,1032,128]{2,1,0:T(8,128)(2,1)}) custom-call(bf16[128,4096]{1,0:T(8,128)(2,1)} %q_ref.1, bf16[128,4096]{1,0:T(8,128)(2,1)} %s_ref.1, bf16[128,4096]{1,0:T(8,128)(2,1)} %g_ref.1), custom_call_target="tpu_custom_call" | custom-call | tf_op jit(solution)/shard_map/pallas_call | solution.py:210
  10.8 1.3 all-to-all-done.2
  12.1 3.5 %all-to-all-start = ((bf16[4,1024,128]{2,1,0:T(8,128)(2,1)}), bf16[4,1024,128]{2,1,0:T(8,128)(2,1)S(1)}, u32[]{:S(2)}, u32[]{:S(2)}) async-start(bf16[4,1024,128]{2,1,0:T(8,128)(2,1)} %get-tuple-element.12), calls=%async_computation | async-start | bytes 2097152 | tf_op jit(solution)/shard_map/all_to_all | solution.py:223
  15.6 8.1 %collective-permute-start = (bf16[2,256,128]{2,1,0:T(8,128)(2,1)S(1)}, bf16[2,256,128]{2,1,0:T(8,128)(2,1)S(1)}, u32[]{:S(2)}, u32[]{:S(2)}) collective-permute-start(bf16[2,256,128]{2,1,0:T(8,128)(2,1)S(1)} %slice.14), channel_id=1, source_target_pairs={{0,16},{16,32},{32,48},{1,17},{17,33},{33,49},{2,18},{18,34},{34,5... | collective-permute-start | bytes 393224 | tf_op jit(solution)/shard_map/ppermute | solution.py:204
  23.7 5.0 %all-to-all-done.q_ref = bf16[4,1024,128]{2,1,0:T(8,128)(2,1)S(1)} async-done(((bf16[4,1024,128]{2,1,0:T(8,128)(2,1)}), bf16[4,1024,128]{2,1,0:T(8,128)(2,1)S(1)}, u32[]{:S(2)}, u32[]{:S(2)}) %all-to-all-start) | async-done | bytes 1048608 | tf_op jit(solution)/shard_map/all_to_all | solution.py:223
  28.7 1.0 copy-done.2
  29.7 3.5 %all-to-all-start.1 = ((bf16[4,1032,128]{2,1,0:T(8,128)(2,1)}), bf16[4,1032,128]{2,1,0:T(8,128)(2,1)S(1)}, u32[]{:S(2)}, u32[]{:S(2)}) async-start(bf16[4,1032,128]{2,1,0:T(8,128)(2,1)} %get-tuple-element.13), calls=%async_computation.1 | async-start | bytes 2113536 | tf_op jit(solution)/shard_map/all_to_all | solution.py:224
  33.2 0.0 collective-permute-done
  33.3 0.0 copy-start
  33.3 0.1 constant_dynamic-slice_fusion
  33.4 0.1 collective-permute-start.3
  33.5 1.0 collective-permute-start.2
  34.5 0.5 collective-permute-start.1
  34.9 4.9 %collective-permute-done.3.y3_ref = bf16[5,256,128]{2,1,0:T(8,128)(2,1)S(1)} collective-permute-done((bf16[5,256,128]{2,1,0:T(8,128)(2,1)S(1)}, bf16[5,256,128]{2,1,0:T(8,128)(2,1)S(1)}, u32[]{:S(2)}, u32[]{:S(2)}) %collective-permute-start.3) | collective-permute-done | bytes 327712 | tf_op jit(solution)/shard_map/ppermute | solution.py:235
  39.8 0.0 copy-start.7
  39.8 20.7 %collective-permute-done.2.y2_ref = bf16[5,256,128]{2,1,0:T(8,128)(2,1)S(1)} collective-permute-done((bf16[5,256,128]{2,1,0:T(8,128)(2,1)S(1)}, bf16[5,256,128]{2,1,0:T(8,128)(2,1)S(1)}, u32[]{:S(2)}, u32[]{:S(2)}) %collective-permute-start.2) | collective-permute-done | bytes 327712 | tf_op jit(solution)/shard_map/ppermute | solution.py:235
  60.5 0.0 collective-permute-done.1.y1_ref
  60.5 0.0 all-to-all-done.1.g_ref
  60.5 0.0 copy-done
  60.5 0.0 copy-done.7
  60.5 0.7 copy-done.8
  61.3 0.1 copy-done.9
  61.4 1.0 copy-done.1
  62.3 25.3 %shard_map.87 = (bf16[4,1024,128]{2,1,0:T(8,128)(2,1)}, f32[6,256,128]{2,1,0:T(8,128)}, bf16[5,256,128]{2,1,0:T(8,128)(2,1)}, bf16[5,256,128]{2,1,0:T(8,128)(2,1)}, bf16[5,256,128]{2,1,0:T(8,128)(2,1)}) custom-call(s32[8]{0:T(128)} %doc_ref.1, bf16[4,1024,128]{2,1,0:T(8,128)(2,1)} %copy-done.2, bf16[4,1032,128]{2,1,0:T(8,128)(2,1)} %copy-done.1, ...), custom_call_target="tpu_custom_call" | custom-call | flops 6039797760 | bytes 8388608 | tf_op jit(solution)/shard_map/pallas_call | solution.py:242
  87.6 0.1 collective-permute-start.4
  87.7 4.5 %collective-permute-start.5 = (bf16[5,256,128]{2,1,0:T(8,128)(2,1)}, bf16[5,256,128]{2,1,0:T(8,128)(2,1)S(1)}, u32[]{:S(2)}, u32[]{:S(2)}) collective-permute-start(bf16[5,256,128]{2,1,0:T(8,128)(2,1)} %get-tuple-element.17), channel_id=1, source_target_pairs={{2,0},{3,1},{0,2},{1,3},{6,4},{7,5},{4,6},{5,7},{10,8},{11,9},{8,1... | collective-permute-start | bytes 983048 | tf_op jit(solution)/shard_map/ppermute | solution.py:282
  92.2 1.4 collective-permute-start.6
  93.6 2.0 %collective-permute-done.4.a_ref = bf16[5,256,128]{2,1,0:T(8,128)(2,1)S(1)} collective-permute-done((bf16[5,256,128]{2,1,0:T(8,128)(2,1)}, bf16[5,256,128]{2,1,0:T(8,128)(2,1)S(1)}, u32[]{:S(2)}, u32[]{:S(2)}) %collective-permute-start.4) | collective-permute-done | bytes 327712 | tf_op jit(solution)/shard_map/ppermute | solution.py:282
  95.6 25.4 %collective-permute-done.5.b_ref = bf16[5,256,128]{2,1,0:T(8,128)(2,1)S(1)} collective-permute-done((bf16[5,256,128]{2,1,0:T(8,128)(2,1)}, bf16[5,256,128]{2,1,0:T(8,128)(2,1)S(1)}, u32[]{:S(2)}, u32[]{:S(2)}) %collective-permute-start.5) | collective-permute-done | bytes 327712 | tf_op jit(solution)/shard_map/ppermute | solution.py:282
  121.0 0.0 collective-permute-done.6.c_ref
  121.0 0.0 copy-done.3
  121.0 0.7 copy-done.4
  121.7 0.1 copy-done.5
  121.8 2.5 %shard_map.88 = (f32[4,256,128]{2,1,0:T(8,128)}, bf16[2,256,128]{2,1,0:T(8,128)(2,1)}) custom-call(f32[6,256,128]{2,1,0:T(8,128)} %get-tuple-element.15.dx_ref, bf16[5,256,128]{2,1,0:T(8,128)(2,1)} %copy-done.3, bf16[5,256,128]{2,1,0:T(8,128)(2,1)} %copy-done.4, bf16[5,256,128]{2,1,0:T(8,128)(2,1)} %copy-done.5), custom_call_target="tpu_custom_call" | custom-call | tf_op jit(solution)/shard_map/pallas_call | solution.py:283
  124.3 3.0 %collective-permute-start.7 = (bf16[2,256,128]{2,1,0:T(8,128)(2,1)}, bf16[2,256,128]{2,1,0:T(8,128)(2,1)S(1)}, u32[]{:S(2)}, u32[]{:S(2)}) collective-permute-start(bf16[2,256,128]{2,1,0:T(8,128)(2,1)} %get-tuple-element.20), channel_id=1, source_target_pairs={{16,0},{32,16},{48,32},{17,1},{33,17},{49,33},{18,2},{34,18},{50,3... | collective-permute-start | bytes 393224 | tf_op jit(solution)/shard_map/ppermute | solution.py:293
  127.3 8.2 %collective-permute-done.7.halo_ref = bf16[2,256,128]{2,1,0:T(8,128)(2,1)S(1)} collective-permute-done((bf16[2,256,128]{2,1,0:T(8,128)(2,1)}, bf16[2,256,128]{2,1,0:T(8,128)(2,1)S(1)}, u32[]{:S(2)}, u32[]{:S(2)}) %collective-permute-start.7) | collective-permute-done | bytes 131104 | tf_op jit(solution)/shard_map/ppermute | solution.py:293
  135.5 0.7 copy-done.6
  136.2 1.8 %shard_map.89 = bf16[4,256,128]{2,1,0:T(8,128)(2,1)} custom-call(f32[4,256,128]{2,1,0:T(8,128)} %get-tuple-element.19.own_ref, bf16[2,256,128]{2,1,0:T(8,128)(2,1)} %copy-done.6), custom_call_target="tpu_custom_call" | custom-call | tf_op jit(solution)/shard_map/pallas_call | solution.py:294
  138.0 9.7 %all_to_all.25 = bf16[4,256,128]{2,1,0:T(8,128)(2,1)S(1)} all-to-all(bf16[4,256,128]{2,1,0:T(8,128)(2,1)} %shard_map.89), channel_id=1, replica_groups=mesh['batch'=4,'blk'=4,'y'=4,'z'=4] {'y'}, dimensions={0} | all-to-all | bytes 524288 | tf_op jit(solution)/shard_map/all_to_all | solution.py:300
  147.7 3.5 %all-to-all-start.3 = ((bf16[4,1024,128]{2,1,0:T(8,128)(2,1)}), bf16[4,1024,128]{2,1,0:T(8,128)(2,1)S(1)}, u32[]{:S(2)}, u32[]{:S(2)}) async-start(bf16[4,1024,128]{2,1,0:T(8,128)(2,1)} %get-tuple-element.14), calls=%async_computation.3 | async-start | bytes 2097152 | tf_op jit(solution)/shard_map/all_to_all | solution.py:277
  151.3 0.1 copy.11
  151.4 0.1 copy.10
  151.5 0.7 copy_bitcast_fusion.1
  152.2 9.5 %all-to-all-done.3 = bf16[4,1024,128]{2,1,0:T(8,128)(2,1)S(1)} async-done(((bf16[4,1024,128]{2,1,0:T(8,128)(2,1)}), bf16[4,1024,128]{2,1,0:T(8,128)(2,1)S(1)}, u32[]{:S(2)}, u32[]{:S(2)}) %all-to-all-start.3) | async-done | bytes 1048608 | tf_op jit(solution)/shard_map/all_to_all | solution.py:277
  161.8 0.7 copy.9
  162.4 1.4 copy.18
  (12 shorter events, 0.1 us)
Async XLA Ops:
  2.3 9.7 %all-to-all-start.2 = ((bf16[4,256,128]{2,1,0:T(8,128)(2,1)}), bf16[4,256,128]{2,1,0:T(8,128)(2,1)S(1)}, u32[]{:S(2)}, u32[]{:S(2)}) async-start(bf16[4,256,128]{2,1,0:T(8,128)(2,1)} %shard_map.86), calls=%async_computation.2 | async-start | bytes 524288 | tf_op jit(solution)/shard_map/all_to_all | solution.py:202
  12.1 16.6 %all-to-all-start = ((bf16[4,1024,128]{2,1,0:T(8,128)(2,1)}), bf16[4,1024,128]{2,1,0:T(8,128)(2,1)S(1)}, u32[]{:S(2)}, u32[]{:S(2)}) async-start(bf16[4,1024,128]{2,1,0:T(8,128)(2,1)} %get-tuple-element.12), calls=%async_computation | async-start | bytes 2097152 | tf_op jit(solution)/shard_map/all_to_all | solution.py:223
  15.6 17.6 %collective-permute-start = (bf16[2,256,128]{2,1,0:T(8,128)(2,1)S(1)}, bf16[2,256,128]{2,1,0:T(8,128)(2,1)S(1)}, u32[]{:S(2)}, u32[]{:S(2)}) collective-permute-start(bf16[2,256,128]{2,1,0:T(8,128)(2,1)S(1)} %slice.14), channel_id=1, source_target_pairs={{0,16},{16,32},{32,48},{1,17},{17,33},{33,49},{2,18},{18,34},{34,5... | collective-permute-start | bytes 393224 | tf_op jit(solution)/shard_map/ppermute | solution.py:204
  28.7 1.0 copy-start.2
  29.7 30.8 %all-to-all-start.1 = ((bf16[4,1032,128]{2,1,0:T(8,128)(2,1)}), bf16[4,1032,128]{2,1,0:T(8,128)(2,1)S(1)}, u32[]{:S(2)}, u32[]{:S(2)}) async-start(bf16[4,1032,128]{2,1,0:T(8,128)(2,1)} %get-tuple-element.13), calls=%async_computation.1 | async-start | bytes 2113536 | tf_op jit(solution)/shard_map/all_to_all | solution.py:224
  33.3 27.2 %copy-start = (bf16[6,256,128]{2,1,0:T(8,128)(2,1)}, bf16[6,256,128]{2,1,0:T(8,128)(2,1)S(1)}, u32[]{:S(2)}) copy-start(bf16[6,256,128]{2,1,0:T(8,128)(2,1)S(1)} %constant_dynamic-update-slice_fusion.x_ref) | copy-start | bytes 1179652
  33.4 6.4 %collective-permute-start.3 = (bf16[5,256,128]{2,1,0:T(8,128)(2,1)S(1)}, bf16[5,256,128]{2,1,0:T(8,128)(2,1)S(1)}, u32[]{:S(2)}, u32[]{:S(2)}) collective-permute-start(bf16[5,256,128]{2,1,0:T(8,128)(2,1)S(1)} %get-tuple-element.21), channel_id=1, source_target_pairs={{0,1},{1,2},{2,3},{3,0},{4,5},{5,6},{6,7},{7,4},{8,9},{9,10},{10,1... | collective-permute-start | bytes 983048 | tf_op jit(solution)/shard_map/ppermute | solution.py:235
  33.5 27.0 %collective-permute-start.2 = (bf16[5,256,128]{2,1,0:T(8,128)(2,1)S(1)}, bf16[5,256,128]{2,1,0:T(8,128)(2,1)S(1)}, u32[]{:S(2)}, u32[]{:S(2)}) collective-permute-start(bf16[5,256,128]{2,1,0:T(8,128)(2,1)S(1)} %get-tuple-element.22), channel_id=1, source_target_pairs={{0,2},{1,3},{2,0},{3,1},{4,6},{5,7},{6,4},{7,5},{8,10},{9,11},{10,... | collective-permute-start | bytes 983048 | tf_op jit(solution)/shard_map/ppermute | solution.py:235
  34.5 26.0 %collective-permute-start.1 = (bf16[5,256,128]{2,1,0:T(8,128)(2,1)S(1)}, bf16[5,256,128]{2,1,0:T(8,128)(2,1)S(1)}, u32[]{:S(2)}, u32[]{:S(2)}) collective-permute-start(bf16[5,256,128]{2,1,0:T(8,128)(2,1)S(1)} %get-tuple-element.23), channel_id=1, source_target_pairs={{0,3},{1,0},{2,1},{3,2},{4,7},{5,4},{6,5},{7,6},{8,11},{9,8},{10,9... | collective-permute-start | bytes 983048 | tf_op jit(solution)/shard_map/ppermute | solution.py:235
  39.8 20.7 %copy-start.7 = (bf16[5,256,128]{2,1,0:T(8,128)(2,1)}, bf16[5,256,128]{2,1,0:T(8,128)(2,1)S(1)}, u32[]{:S(2)}) copy-start(bf16[5,256,128]{2,1,0:T(8,128)(2,1)S(1)} %collective-permute-done.3.y3_ref) | copy-start | bytes 983044
  60.5 0.7 copy-start.8
  60.5 0.9 copy-start.9
  61.4 1.0 copy-start.1
  87.6 8.0 %collective-permute-start.4 = (bf16[5,256,128]{2,1,0:T(8,128)(2,1)}, bf16[5,256,128]{2,1,0:T(8,128)(2,1)S(1)}, u32[]{:S(2)}, u32[]{:S(2)}) collective-permute-start(bf16[5,256,128]{2,1,0:T(8,128)(2,1)} %get-tuple-element.16), channel_id=1, source_target_pairs={{3,0},{0,1},{1,2},{2,3},{7,4},{4,5},{5,6},{6,7},{11,8},{8,9},{9,10... | collective-permute-start | bytes 983048 | tf_op jit(solution)/shard_map/ppermute | solution.py:282
  87.7 33.3 %collective-permute-start.5 = (bf16[5,256,128]{2,1,0:T(8,128)(2,1)}, bf16[5,256,128]{2,1,0:T(8,128)(2,1)S(1)}, u32[]{:S(2)}, u32[]{:S(2)}) collective-permute-start(bf16[5,256,128]{2,1,0:T(8,128)(2,1)} %get-tuple-element.17), channel_id=1, source_target_pairs={{2,0},{3,1},{0,2},{1,3},{6,4},{7,5},{4,6},{5,7},{10,8},{11,9},{8,1... | collective-permute-start | bytes 983048 | tf_op jit(solution)/shard_map/ppermute | solution.py:282
  92.2 28.8 %collective-permute-start.6 = (bf16[5,256,128]{2,1,0:T(8,128)(2,1)}, bf16[5,256,128]{2,1,0:T(8,128)(2,1)S(1)}, u32[]{:S(2)}, u32[]{:S(2)}) collective-permute-start(bf16[5,256,128]{2,1,0:T(8,128)(2,1)} %get-tuple-element.18), channel_id=1, source_target_pairs={{1,0},{2,1},{3,2},{0,3},{5,4},{6,5},{7,6},{4,7},{9,8},{10,9},{11,1... | collective-permute-start | bytes 983048 | tf_op jit(solution)/shard_map/ppermute | solution.py:282
  95.6 25.4 %copy-start.3 = (bf16[5,256,128]{2,1,0:T(8,128)(2,1)}, bf16[5,256,128]{2,1,0:T(8,128)(2,1)S(1)}, u32[]{:S(2)}) copy-start(bf16[5,256,128]{2,1,0:T(8,128)(2,1)S(1)} %collective-permute-done.4.a_ref) | copy-start | bytes 983044
  121.0 0.7 copy-start.4
  121.0 0.8 copy-start.5
  124.3 11.2 %collective-permute-start.7 = (bf16[2,256,128]{2,1,0:T(8,128)(2,1)}, bf16[2,256,128]{2,1,0:T(8,128)(2,1)S(1)}, u32[]{:S(2)}, u32[]{:S(2)}) collective-permute-start(bf16[2,256,128]{2,1,0:T(8,128)(2,1)} %get-tuple-element.20), channel_id=1, source_target_pairs={{16,0},{32,16},{48,32},{17,1},{33,17},{49,33},{18,2},{34,18},{50,3... | collective-permute-start | bytes 393224 | tf_op jit(solution)/shard_map/ppermute | solution.py:293
  135.5 0.7 copy-start.6
  147.7 14.1 %all-to-all-start.3 = ((bf16[4,1024,128]{2,1,0:T(8,128)(2,1)}), bf16[4,1024,128]{2,1,0:T(8,128)(2,1)S(1)}, u32[]{:S(2)}, u32[]{:S(2)}) async-start(bf16[4,1024,128]{2,1,0:T(8,128)(2,1)} %get-tuple-element.14), calls=%async_computation.3 | async-start | bytes 2097152 | tf_op jit(solution)/shard_map/all_to_all | solution.py:277
